TPU v7x, 128 devices: a whole 4x4x4 slice. The times are simulated.
128 devices in a mesh: grp: 8 (over x_lo, z), row: 16 (over x_hi, y, core).
Axes of the slice: x: 4 (x_hi: 2, x_lo: 2; x = x_hi * 2 + x_lo), y: 4, z: 4, core: 2. Of those that a mesh axis runs over, the one named last changes fastest.
Arguments:
- probes: bfloat16 [8, 8192, 2048], P('grp', 'row'), may hold values from -6 to 6
- solves: bfloat16 [8, 8192, 2048], P('grp', 'row'), may hold values from -6 to 6
- row_spectra: float32 [8, 8192], replicated, may hold values from -0.0625 to 0.0625
- col_spectra: float32 [8, 2048], replicated, may hold values from -0.125 to 0.125
Outputs:
- row_traces: float32 [8, 8192], P(None, ('grp', 'row'))
- col_traces: float32 [8, 2048], replicated
All inputs are finite; a program needn't handle non-finite values.
Results may differ from a plain program's by a relative error of at most 0.0003.
Values sent between devices are 32-bit elements; how exact they have to be, the bound alone decides.
A program may use at most 128 MiB of HBM per device.

v0:
```python
import functools
import math

import jax
import jax.numpy as jnp
import ml_dtypes
import numpy as np
from jax import lax
from jax.experimental import pallas as pl
from jax.experimental.pallas import tpu as pltpu
from jax.sharding import PartitionSpec as P

L1, L2, HYPER, PROBES = 8192, 2048, 8, 8
ROWS, GRPS = 16, 8
LOCAL = L1 // ROWS
CH = 4
CR = LOCAL // CH
F32, BF16 = jnp.float32, jnp.bfloat16
MESH = pl.DeviceIdType.MESH
SCALE = 1.0 / (PROBES * L1 * L2)
NT = (((1,), (1,)), ((), ()))
NN = (((1,), (0,)), ((), ()))


def halves(table):
    hi = table.astype(ml_dtypes.bfloat16)
    lo = (table - hi.astype(np.float64)).astype(ml_dtypes.bfloat16)
    return hi, lo


@functools.lru_cache(maxsize=None)
def tables():
    x = np.arange(L2)
    w = np.zeros((8, 2, L2, 256), ml_dtypes.bfloat16)
    for pair in range(8):
        for t in range(2):
            j = (2 * pair + t) * 64 + np.arange(64)
            ang = 2 * math.pi * (x[:, None] * j[None, :] % L2) / L2
            hi, lo = halves(np.concatenate([np.cos(ang), -np.sin(ang)], 1))
            w[pair, 0, :, t * 128 : t * 128 + 128] = hi
            w[pair, 1, :, t * 128 : t * 128 + 128] = lo
    fh = np.arange(LOCAL)
    d = np.zeros((CH, 2, LOCAL, 2 * CR), ml_dtypes.bfloat16)
    for c in range(CH):
        r = c * CR + np.arange(CR)
        ang = 2 * math.pi * (fh[:, None] * r[None, :] % LOCAL) / LOCAL
        d[c, 0], d[c, 1] = halves(np.concatenate([np.cos(ang), np.sin(ang)], 1))
    r = np.arange(LOCAL)
    tw = np.zeros((LOCAL, 128), np.float32)
    for f in range(16):
        ang = 2 * math.pi * (r * f % L1) / L1
        tw[:, 2 * f], tw[:, 2 * f + 1] = np.cos(ang), np.sin(ang)
    tb = np.zeros((16, 64, 128), np.float32)
    for f in range(16):
        for dd in range(16):
            tb[f, 2 * dd] = math.cos(2 * math.pi * (dd * f % 16) / 16)
            tb[f, 2 * dd + 1] = math.sin(2 * math.pi * (dd * f % 16) / 16)
        for q in range(4):
            ang = 2 * math.pi * ((q * 128 + np.arange(128)) * f % L1) / L1
            for zu in range(2):
                tb[f, 32 + zu * 4 + q] = np.cos(ang)
                tb[f, 40 + zu * 4 + q] = np.sin(ang)
    return w, d, tw, tb


def split(v):
    hi = v.astype(BF16)
    return hi, (v - hi.astype(F32)).astype(BF16)


def mm(a, b, dims=NN):
    return lax.dot_general(a, b, dims, preferred_element_type=F32)


def exact(a, b):
    return lax.dot_general(a, b, NN, precision=lax.Precision.HIGHEST, preferred_element_type=F32)


def minus_i(v, sign):
    return pltpu.roll(v, 64, axis=1) * sign


def turn(v, m, sign):
    m = m % 16
    if m == 0:
        return v
    if m == 4:
        return minus_i(v, sign)
    return v * math.cos(2 * math.pi * m / 16) + minus_i(v, sign) * math.sin(2 * math.pi * m / 16)


def four(a, b, c, d, sign):
    s, t, u = a + c, a - c, b + d
    v = minus_i(b - d, sign)
    return s + u, t + v, s - u, t - v


def kernel(
    z_hbm, u_hbm, rs_hbm, cs_hbm, w_hbm, d_hbm, tw_hbm, tb_hbm,
    row_ref, col_ref,
    x, wbuf, dt, tw, tb, rs, cs, send, recv, acc, yh, yl, cross,
    bs, brecv, lb, upm, r32, tiles, mir, pex, qb, r1, q1, r2s, r2, q2s, q2,
    lsem, wsem, ssem, rsem, own, bss, brs, e1s, e1r, f1s, f1r, e2s, e2r, f2s, f2r,
):
    me, g = lax.axis_index("row"), lax.axis_index("grp")
    xh, y, core = me // 8, (me // 2) % 4, me % 2
    barrier = pltpu.get_barrier_semaphore()
    for k in range(1, ROWS):
        pl.semaphore_signal(barrier, inc=1, device_id={"row": lax.rem(me + k, ROWS)}, device_id_type=MESH)
    for k in range(1, GRPS):
        pl.semaphore_signal(barrier, inc=1, device_id={"grp": lax.rem(g + k, GRPS)}, device_id_type=MESH)

    def pair_of(s):
        o = s + 1
        return lax.rem(xh + lax.rem(o, 2), 2) * 4 + lax.rem(y + lax.rem(o // 2, 4), 4)

    def w_copy(s, slot):
        return pltpu.make_async_copy(w_hbm.at[pair_of(s)], wbuf.at[slot], wsem.at[slot])

    loads = [
        pltpu.make_async_copy(z_hbm.at[0], x.at[0], lsem.at[0]),
        pltpu.make_async_copy(u_hbm.at[0], x.at[1], lsem.at[1]),
        pltpu.make_async_copy(d_hbm, dt, lsem.at[2]),
        pltpu.make_async_copy(tw_hbm, tw, lsem.at[3]),
        pltpu.make_async_copy(tb_hbm.at[me], tb, lsem.at[4]),
        pltpu.make_async_copy(rs_hbm, rs, lsem.at[5]),
        pltpu.make_async_copy(cs_hbm, cs, lsem.at[6]),
    ]
    loads[0].start()
    w_copy(0, 0).start()
    for cp in loads[1:]:
        cp.start()

    def block(s, t, c):
        return pltpu.make_async_remote_copy(
            src_ref=send.at[s, t, c], dst_ref=recv.at[me, c], send_sem=ssem.at[c, 2 * s + t],
            recv_sem=rsem.at[c, me], device_id={"row": 2 * pair_of(s) + t}, device_id_type=MESH,
        )

    def arrival(c, d):
        return pltpu.make_async_remote_copy(
            src_ref=send.at[0, 0, c], dst_ref=recv.at[d, c], send_sem=ssem.at[c, 0],
            recv_sem=rsem.at[c, d], device_id={"row": d}, device_id_type=MESH,
        )

    def start_block(s, c):
        @pl.when(s < 7)
        def _():
            block(s, 0, c).start()
            block(s, 1, c).start()

        @pl.when(s == 7)
        def _():
            block(7, 1 - core, c).start()

    loads[0].wait()
    loads[1].wait()
    pl.semaphore_wait(barrier, ROWS - 1 + GRPS - 1)

    def section(s, _):
        slot = lax.rem(s, 2)
        w_copy(s, slot).wait()

        @pl.when(s < 7)
        def _():
            w_copy(s + 1, 1 - slot).start()

        for zu in range(2):
            got = mm(x[zu], wbuf[slot, 0]) + mm(x[zu], wbuf[slot, 1])
            for t in range(2):
                for c in range(CH):
                    send[s, t, c, pl.ds(zu * CR, CR)] = got[c * CR : (c + 1) * CR, t * 128 : (t + 1) * 128]
        start_block(s, 0)
        return 0

    lax.fori_loop(0, 8, section, 0)
    mine = pltpu.make_async_copy(send.at[7, core], recv.at[me], own)
    mine.start()

    lane = lax.broadcasted_iota(jnp.int32, (8, 128), 1)
    sub = lax.broadcasted_iota(jnp.int32, (128, 128), 0)
    lan = lax.broadcasted_iota(jnp.int32, (128, 128), 1)
    parity = lax.broadcasted_iota(jnp.int32, (L2, 128), 0) % 2
    alt = (1 - 2 * parity).astype(F32).astype(BF16)
    for zu in range(2):
        summed = mm(x[zu], alt)
        for q in range(4):
            bs[pl.ds(zu * 4 + q, 1)] = jnp.sum(
                jnp.where(sub == lan, summed[q * 128 : (q + 1) * 128], 0.0), axis=0, keepdims=True
            )

    def b_copy(k):
        return pltpu.make_async_remote_copy(
            src_ref=bs, dst_ref=brecv.at[me], send_sem=bss.at[k], recv_sem=brs.at[me],
            device_id={"row": lax.rem(me + k, ROWS)}, device_id_type=MESH,
        )

    for k in range(1, ROWS):
        b_copy(k).start()
    for c in range(1, CH):
        lax.fori_loop(0, 8, lambda s, _, c=c: (start_block(s, c), 0)[1], 0)

    for cp in loads[2:]:
        cp.wait()
    flip = (lax.rem(sub + lan, 128) == 0).astype(F32)

    def stack_r(t, _):
        tiles[t] = rs[:, pl.ds(pl.multiple_of(t * 128, 128), 128)]
        return 0

    lax.fori_loop(0, 64, stack_r, 0)
    mir[...] = exact(tiles[...].reshape(512, 128), flip).reshape(64, 8, 128)

    def put_r(t, _):
        back = jnp.where(lane == 0, mir[lax.rem(64 - t, 64)], mir[63 - t])
        both = jnp.concatenate([tiles[t], back], axis=0)
        hi, lo = split(both)
        at = pl.ds(pl.multiple_of(t * 128, 128), 128)
        r32[pl.ds(0, 16), at] = hi
        r32[pl.ds(16, 16), at] = lo
        return 0

    lax.fori_loop(0, 64, put_r, 0)

    def own_half(tile):
        other = pltpu.roll(tile, 64, axis=1)
        low = lane < 64
        return jnp.where(core == 0, jnp.where(low, tile, other), jnp.where(low, other, tile))

    at = me // 2
    c_here = cs[:, pl.ds(pl.multiple_of(at * 128, 128), 128)]
    c_a = cs[:, pl.ds(pl.multiple_of((15 - at) * 128, 128), 128)]
    c_b = cs[:, pl.ds(pl.multiple_of(lax.rem(16 - at, 16) * 128, 128), 128)]
    c_back = jnp.where(lane == 0, exact(c_b, flip), exact(c_a, flip))
    c_back = own_half(c_back)
    c_back = jnp.where(jnp.logical_and(me == 0, lax.rem(lane, 64) == 0), 0.0, c_back)
    c_hi, c_lo = split(jnp.concatenate([own_half(c_here), c_back], axis=0))
    c_both = jnp.concatenate([c_hi, c_lo], axis=0)

    for k in range(1, ROWS):
        d = lax.rem(me + k, ROWS)
        pltpu.make_async_remote_copy(
            src_ref=bs, dst_ref=brecv.at[d], send_sem=bss.at[0], recv_sem=brs.at[d],
            device_id={"row": d}, device_id_type=MESH,
        ).wait_recv()
    brecv[me] = bs[...]
    re = jnp.zeros((8, 128), F32)
    im = jnp.zeros((8, 128), F32)
    for d in range(ROWS):
        re = re + brecv[d] * tb[pl.ds(2 * d, 1)]
        im = im - brecv[d] * tb[pl.ds(2 * d + 1, 1)]
    tc, ts = tb[pl.ds(32, 8)], tb[pl.ds(40, 8)]
    bs2_re = re * tc + im * ts
    bs2_im = im * tc - re * ts
    lb[...] = jnp.zeros_like(lb)
    for q in range(4):
        for zu in range(2):
            a = bs2_re[zu * 4 + q : zu * 4 + q + 1]
            b = bs2_im[zu * 4 + q : zu * 4 + q + 1]
            lb[pl.ds(zu, 1), pl.ds(q * 256, 128)] = a
            lb[pl.ds(zu, 1), pl.ds(q * 256 + 128, 128)] = b
            lb[pl.ds(2 + zu, 1), pl.ds(q * 256, 128)] = b
            lb[pl.ds(2 + zu, 1), pl.ds(q * 256 + 128, 128)] = -a
    mid = jnp.zeros((16, LOCAL), F32)
    for q in range(4):
        hi, lo = split(lb[:, q * 256 : (q + 1) * 256])
        mid = mid + mm(hi, dt[q, 0], NT) + mm(lo, dt[q, 0], NT) + mm(hi, dt[q, 1], NT)
    mid_cross = mid[0:1] * mid[1:2] + mid[2:3] * mid[3:4]
    lb[...] = jnp.zeros_like(lb)
    for q in range(4):
        lb[pl.ds(q, 1), pl.ds(0, 128)] = mid_cross[:, q * 128 : (q + 1) * 128]
    spread = (
        lax.broadcasted_iota(jnp.int32, (128, 2048), 1) == 16 * lax.broadcasted_iota(jnp.int32, (128, 2048), 0) + me
    ).astype(F32)
    upm[...] = exact(lb[pl.ds(0, 8), pl.ds(0, 128)], spread)
    c_mid = jnp.broadcast_to(cs[:, 1024:1025], (8, 128))
    total = jnp.zeros((8, 128), F32)
    for q in range(4):

        def put_mid(t, total, q=q):
            up = upm[pl.ds(q, 1), pl.ds(pl.multiple_of(t * 128, 128), 128)]
            pex[q * 16 + t] = c_mid * up
            return total + tiles[q * 16 + t] * up

        total = lax.fori_loop(0, 16, put_mid, total)
    qb[pl.ds(16, 8)] = jnp.broadcast_to(jnp.sum(total, axis=1, keepdims=True), (8, 128))

    sign = jnp.where(lax.broadcasted_iota(jnp.int32, (16, 128), 1) < 64, 1.0, -1.0).astype(F32)
    mine.wait()

    def turned(c):
        for k in range(1, ROWS):
            arrival(c, lax.rem(me + k, ROWS)).wait_recv()

        def rows16(i, _):
            at = pl.ds(pl.multiple_of(i * 16, 16), 16)
            jat = pl.ds(pl.multiple_of(CR + i * 16, 16), 16)
            coef = tw[pl.ds(pl.multiple_of(c * CR + i * 16, 16), 16)]
            for zu in range(2):
                v = [recv[d, c, pl.ds(pl.multiple_of(zu * CR + i * 16, 16), 16)] for d in range(ROWS)]
                inner = [four(v[d0], v[d0 + 4], v[d0 + 8], v[d0 + 12], sign) for d0 in range(4)]
                for f0 in range(4):
                    outs = four(*[turn(inner[d0][f0], d0 * f0, sign) for d0 in range(4)], sign)
                    for f1 in range(4):
                        f = f0 + 4 * f1
                        val = outs[f1]
                        jval = minus_i(val, sign)
                        if f:
                            cc = jnp.broadcast_to(coef[:, 2 * f : 2 * f + 1], (16, 128))
                            ss = jnp.broadcast_to(coef[:, 2 * f + 1 : 2 * f + 2], (16, 128))
                            val, jval = val * cc + jval * ss, jval * cc - val * ss
                        cols = pl.ds(f * 256 + zu * 128, 128)
                        yh[at, cols], yl[at, cols] = split(val)
                        yh[jat, cols], yl[jat, cols] = split(jval)
            return 0

        lax.fori_loop(0, CR // 16, rows16, 0)

    def product(c, cols):
        a, b = yh[:, cols], yl[:, cols]
        return mm(dt[c, 0], a) + mm(dt[c, 0], b) + mm(dt[c, 1], a)

    for c in range(CH - 1):
        turned(c)

        def add(n, _, c=c):
            cols = pl.ds(pl.multiple_of(n * 512, 512), 512)
            got = product(c, cols)
            acc[:, cols] = got if c == 0 else acc[:, cols] + got
            return 0

        lax.fori_loop(0, 8, add, 0)

    turned(CH - 1)

    def finish(n, _):
        cols = pl.ds(pl.multiple_of(n * 512, 512), 512)
        got = acc[:, cols] + product(CH - 1, cols)
        for h in range(2):
            cross[pl.ds(2 * n + h, LOCAL, stride=16)] = (
                got[:, h * 256 : h * 256 + 128] * got[:, h * 256 + 128 : h * 256 + 256]
            )
        return 0

    lax.fori_loop(0, 8, finish, 0)

    def contract(n, q):
        at = pl.ds(pl.multiple_of(n * 512, 512), 512)
        hi, lo = split(cross[at])
        a = mm(c_both, hi, NT)
        p = a[:16] + a[16:] + mm(c_hi, lo, NT)
        for i in range(4):
            pex[n * 4 + i] = pex[n * 4 + i] + p[:8, i * 128 : (i + 1) * 128]
            tiles[n * 4 + i] = p[8:, i * 128 : (i + 1) * 128]
        weights = r32[:, at]
        b = mm(weights, hi)
        return q + b[:16] + b[16:] + mm(weights[:16], lo)

    qb[pl.ds(0, 16)] = lax.fori_loop(0, 16, contract, jnp.zeros((16, 128), F32))
    mir[...] = exact(tiles[...].reshape(512, 128), flip).reshape(64, 8, 128)

    def join(t, _):
        back = jnp.where(lane == 0, mir[lax.rem(64 - t, 64)], mir[63 - t])
        pex[t] = (pex[t] + back) * SCALE
        return 0

    lax.fori_loop(0, 64, join, 0)
    qb[...] = qb[...] * SCALE

    def grp_copies(k):
        to = lax.rem(g + k, GRPS)
        return (
            pltpu.make_async_remote_copy(
                src_ref=pex.at[pl.ds(to * 8, 8)], dst_ref=r1.at[g], send_sem=e1s.at[k], recv_sem=e1r.at[g],
                device_id={"grp": to}, device_id_type=MESH,
            ),
            pltpu.make_async_remote_copy(
                src_ref=qb, dst_ref=q1.at[g], send_sem=f1s.at[k], recv_sem=f1r.at[g],
                device_id={"grp": to}, device_id_type=MESH,
            ),
        )

    def grp_arrivals(k):
        d = lax.rem(g + k, GRPS)
        return (
            pltpu.make_async_remote_copy(
                src_ref=pex.at[pl.ds(0, 8)], dst_ref=r1.at[d], send_sem=e1s.at[0], recv_sem=e1r.at[d],
                device_id={"grp": d}, device_id_type=MESH,
            ),
            pltpu.make_async_remote_copy(
                src_ref=qb, dst_ref=q1.at[d], send_sem=f1s.at[0], recv_sem=f1r.at[d],
                device_id={"grp": d}, device_id_type=MESH,
            ),
        )

    for k in range(1, GRPS):
        for cp in grp_copies(k):
            cp.start()
    r1[g] = pex[pl.ds(g * 8, 8)]
    q1[g] = qb[...]
    for k in range(1, GRPS):
        for cp in grp_arrivals(k):
            cp.wait_recv()
    r2s[...] = functools.reduce(lambda a, d: a + r1[d], range(1, GRPS), r1[0])
    q2s[...] = functools.reduce(lambda a, d: a + q1[d], range(1, GRPS), q1[0])

    def row_copies(k):
        to = lax.rem(me + k, ROWS)
        return (
            pltpu.make_async_remote_copy(
                src_ref=r2s.at[to // 2], dst_ref=r2.at[me], send_sem=e2s.at[k], recv_sem=e2r.at[me],
                device_id={"row": to}, device_id_type=MESH,
            ),
            pltpu.make_async_remote_copy(
                src_ref=q2s, dst_ref=q2.at[me], send_sem=f2s.at[k], recv_sem=f2r.at[me],
                device_id={"row": to}, device_id_type=MESH,
            ),
        )

    def row_arrivals(k):
        d = lax.rem(me + k, ROWS)
        return (
            pltpu.make_async_remote_copy(
                src_ref=r2s.at[0], dst_ref=r2.at[d], send_sem=e2s.at[0], recv_sem=e2r.at[d],
                device_id={"row": d}, device_id_type=MESH,
            ),
            pltpu.make_async_remote_copy(
                src_ref=q2s, dst_ref=q2.at[d], send_sem=f2s.at[0], recv_sem=f2r.at[d],
                device_id={"row": d}, device_id_type=MESH,
            ),
        )

    for k in range(1, ROWS):
        for cp in row_copies(k):
            cp.start()
    r2[me] = r2s[me // 2]
    q2[me] = q2s[...]
    for k in range(1, ROWS):
        for cp in row_arrivals(k):
            cp.wait_recv()
    tile = functools.reduce(lambda a, d: a + r2[d], range(1, ROWS), r2[0])
    row_ref[...] = jnp.where(core == 0, tile, pltpu.roll(tile, 64, axis=1))[:, :64]
    low = lax.broadcasted_iota(jnp.int32, (16, 128), 1) < 64
    middle = functools.reduce(lambda a, d: a + q2[d, pl.ds(16, 8)], range(1, ROWS), q2[0, pl.ds(16, 8)])
    for m in range(8):
        a, b = q2[2 * m, pl.ds(0, 16)], q2[2 * m + 1, pl.ds(0, 16)]
        ab = jnp.where(low, a + pltpu.roll(a, 64, axis=1), b + pltpu.roll(b, 64, axis=1))
        col_ref[:, pl.ds(m * 128, 128)] = ab[:8]
        tiles[m] = ab[8:]
    mir[pl.ds(0, 8)] = exact(tiles[pl.ds(0, 8)].reshape(64, 128), flip).reshape(8, 8, 128)
    for t in range(8, 16):
        first = middle if t == 8 else mir[16 - t]
        col_ref[:, pl.ds(t * 128, 128)] = jnp.where(lane == 0, first, mir[15 - t])

    for c in range(CH):

        def drain(s, _, c=c):
            @pl.when(s < 7)
            def _():
                block(s, 0, c).wait_send()
                block(s, 1, c).wait_send()

            @pl.when(s == 7)
            def _():
                block(7, 1 - core, c).wait_send()

            return 0

        lax.fori_loop(0, 8, drain, 0)
    for k in range(1, ROWS):
        b_copy(k).wait_send()
        for cp in row_copies(k):
            cp.wait_send()
    for k in range(1, GRPS):
        for cp in grp_copies(k):
            cp.wait_send()


def local(probes, solves, row_spectra, col_spectra):
    w, d, tw, tb = (jnp.asarray(t) for t in tables())
    dma = pltpu.SemaphoreType.DMA
    vm = pltpu.VMEM
    scratch = [
        vm((2, LOCAL, L2), BF16), vm((2, 2, L2, 256), BF16), vm((CH, 2, LOCAL, 2 * CR), BF16),
        vm((LOCAL, 128), F32), vm((64, 128), F32), vm((8, L1), F32), vm((8, L2), F32),
        vm((8, 2, CH, 2 * CR, 128), F32), vm((ROWS, CH, 2 * CR, 128), F32),
        vm((LOCAL, 4096), F32), vm((2 * CR, 4096), BF16), vm((2 * CR, 4096), BF16), vm((L1, 128), F32),
        vm((8, 128), F32), vm((ROWS, 8, 128), F32), vm((16, 1024), F32), vm((8, 2048), F32),
        vm((32, L1), BF16), vm((64, 8, 128), F32), vm((64, 8, 128), F32), vm((64, 8, 128), F32), vm((24, 128), F32),
        vm((GRPS, 8, 8, 128), F32), vm((GRPS, 24, 128), F32), vm((8, 8, 128), F32), vm((ROWS, 8, 128), F32),
        vm((24, 128), F32), vm((ROWS, 24, 128), F32),
        dma((7,)), dma((2,)), dma((CH, ROWS)), dma((CH, ROWS)), dma, dma((ROWS,)), dma((ROWS,)),
        dma((GRPS,)), dma((GRPS,)), dma((GRPS,)), dma((GRPS,)),
        dma((ROWS,)), dma((ROWS,)), dma((ROWS,)), dma((ROWS,)),
    ]
    hbm = pl.BlockSpec(memory_space=pl.ANY)
    return pl.pallas_call(
        kernel,
        out_shape=(jax.ShapeDtypeStruct((HYPER, 64), F32), jax.ShapeDtypeStruct((HYPER, L2), F32)),
        in_specs=[hbm] * 8,
        out_specs=(pl.BlockSpec(memory_space=pltpu.VMEM), pl.BlockSpec(memory_space=pltpu.VMEM)),
        scratch_shapes=scratch,
        compiler_params=pltpu.CompilerParams(collective_id=0, has_side_effects=True, vmem_limit_bytes=62 << 20),
        name="trace_terms",
    )(probes, solves, row_spectra, col_spectra, w, d, tw, tb)


def solution(mesh):
    placed = (P("grp", "row", None), P("grp", "row", None), P(), P())
    return jax.shard_map(
        local, mesh=mesh, in_specs=placed, out_specs=(P(None, ("grp", "row")), P()), check_vma=False
    )
```

profile of v0, /device:TPU:1, one launch (start us, length us, event | category | flops | bytes accessed | tf_op | source)
XLA Modules:
  0.0 143.4 jit_solution(6555767181539635962)
XLA Ops:
  0.6 140.0 %trace_terms.1 = (f32[8,64]{1,0:T(8,128)}, f32[8,2048]{1,0:T(8,128)}) custom-call(bf16[1,512,2048]{2,1,0:T(8,128)(2,1)} %z_hbm.1, bf16[1,512,2048]{2,1,0:T(8,128)(2,1)} %u_hbm.1, f32[8,8192]{1,0:T(8,128)} %rs_hbm.1, f32[8,2048]{1,0:T(8,128)} %cs_hbm.1, bf16[8,2,2048,256]{3,2,1,0:T(8,128)(2,1)} %constant.8.clone.w_hbm, ...), custom_call_target="tpu_custom_call" | custom-call | tf_op jit(solution)/shard_map/trace_terms/pallas_call | solution.py:497
  140.6 1.3 copy.12
  141.9 1.5 %copy.13 = f32[8,2048]{1,0:T(8,128)} copy(f32[8,2048]{1,0:T(8,128)} %get-tuple-element.5) | data formatting | bytes 131072
where the time goes:
time: 144 us; the launch traced here: 143 us
  Pallas kernels  140 us (97%)
  local copies, waits for them, and re-layouts  2.74 us (2%)
    pallas_call x1, Pallas kernels, local(): pl.pallas_call(kernel, out_shape=(jax.ShapeDtypeStruct((HYPER, 64), F32),...  140 us

commit v1 on v0

--- a/solution.py
+++ b/solution.py
@@ -13,8 +13,11 @@
 L1, L2, HYPER, PROBES = 8192, 2048, 8, 8
 ROWS, GRPS = 16, 8
 LOCAL = L1 // ROWS
-CH = 4
-CR = LOCAL // CH
+SIZES = (128, 128, 128, 64, 32, 32)
+STARTS = tuple(sum(SIZES[:c]) for c in range(len(SIZES)))
+CH = len(SIZES)
+WIDTHS = tuple((6 if n == 128 else 8) * n for n in SIZES) + (512,)
+OFFS = tuple(sum(WIDTHS[:c]) for c in range(len(WIDTHS)))
 F32, BF16 = jnp.float32, jnp.bfloat16
 MESH = pl.DeviceIdType.MESH
 SCALE = 1.0 / (PROBES * L1 * L2)
@@ -40,11 +43,13 @@
             w[pair, 0, :, t * 128 : t * 128 + 128] = hi
             w[pair, 1, :, t * 128 : t * 128 + 128] = lo
     fh = np.arange(LOCAL)
-    d = np.zeros((CH, 2, LOCAL, 2 * CR), ml_dtypes.bfloat16)
-    for c in range(CH):
-        r = c * CR + np.arange(CR)
+    d = np.zeros((LOCAL, sum(WIDTHS)), ml_dtypes.bfloat16)
+    for c, (first, n) in enumerate(zip(STARTS + (384,), SIZES + (128,))):
+        r = first + np.arange(n)
         ang = 2 * math.pi * (fh[:, None] * r[None, :] % LOCAL) / LOCAL
-        d[c, 0], d[c, 1] = halves(np.concatenate([np.cos(ang), np.sin(ang)], 1))
+        hi, lo = halves(np.concatenate([np.cos(ang), np.sin(ang)], 1))
+        parts = [hi, lo] if c == CH else [hi, hi, lo] if n == 128 else [hi, hi, lo, lo]
+        d[:, OFFS[c] : OFFS[c] + WIDTHS[c]] = np.concatenate(parts, 1)
     r = np.arange(LOCAL)
     tw = np.zeros((LOCAL, 128), np.float32)
     for f in range(16):
@@ -98,9 +103,9 @@
 def kernel(
     z_hbm, u_hbm, rs_hbm, cs_hbm, w_hbm, d_hbm, tw_hbm, tb_hbm,
     row_ref, col_ref,
-    x, wbuf, dt, tw, tb, rs, cs, send, recv, acc, yh, yl, cross,
-    bs, brecv, lb, upm, r32, tiles, mir, pex, qb, r1, q1, r2s, r2, q2s, q2,
-    lsem, wsem, ssem, rsem, own, bss, brs, e1s, e1r, f1s, f1r, e2s, e2r, f2s, f2r,
+    x, wbuf, dt, tw, tb, rs, cs, send, recv, acc, yy, cross,
+    bs, brecv, ms, mrecv, lb, upm, r32, tiles, mir, pex, qb, r1, q1, r2s, r2, q2s, q2,
+    lsem, wsem, ssem, rsem, own, bss, brs, mss, mrs, e1s, e1r, f1s, f1r, e2s, e2r, f2s, f2r,
 ):
     me, g = lax.axis_index("row"), lax.axis_index("grp")
     xh, y, core = me // 8, (me // 2) % 4, me % 2
@@ -111,8 +116,9 @@
         pl.semaphore_signal(barrier, inc=1, device_id={"grp": lax.rem(g + k, GRPS)}, device_id_type=MESH)
 
     def pair_of(s):
-        o = s + 1
-        return lax.rem(xh + lax.rem(o, 2), 2) * 4 + lax.rem(y + lax.rem(o // 2, 4), 4)
+        m = s % 4
+        dy = (2 + 3 * m + 3 * (m * (m - 1) // 2)) % 4
+        return lax.rem(xh + 1 - s // 4, 2) * 4 + lax.rem(y + dy, 4)
 
     def w_copy(s, slot):
         return pltpu.make_async_copy(w_hbm.at[pair_of(s)], wbuf.at[slot], wsem.at[slot])
@@ -128,18 +134,20 @@
     ]
     loads[0].start()
     w_copy(0, 0).start()
-    for cp in loads[1:]:
-        cp.start()
+    loads[1].start()
+
+    def span(c):
+        return pl.ds(2 * STARTS[c], 2 * SIZES[c])
 
     def block(s, t, c):
         return pltpu.make_async_remote_copy(
-            src_ref=send.at[s, t, c], dst_ref=recv.at[me, c], send_sem=ssem.at[c, 2 * s + t],
+            src_ref=send.at[s, t, span(c)], dst_ref=recv.at[me, span(c)], send_sem=ssem.at[c, 2 * s + t],
             recv_sem=rsem.at[c, me], device_id={"row": 2 * pair_of(s) + t}, device_id_type=MESH,
         )
 
     def arrival(c, d):
         return pltpu.make_async_remote_copy(
-            src_ref=send.at[0, 0, c], dst_ref=recv.at[d, c], send_sem=ssem.at[c, 0],
+            src_ref=send.at[0, 0, span(c)], dst_ref=recv.at[d, span(c)], send_sem=ssem.at[c, 0],
             recv_sem=rsem.at[c, d], device_id={"row": d}, device_id_type=MESH,
         )
 
@@ -169,11 +177,14 @@
             got = mm(x[zu], wbuf[slot, 0]) + mm(x[zu], wbuf[slot, 1])
             for t in range(2):
                 for c in range(CH):
-                    send[s, t, c, pl.ds(zu * CR, CR)] = got[c * CR : (c + 1) * CR, t * 128 : (t + 1) * 128]
+                    first, n = STARTS[c], SIZES[c]
+                    send[s, t, pl.ds(2 * first + zu * n, n)] = got[first : first + n, t * 128 : (t + 1) * 128]
         start_block(s, 0)
         return 0
 
     lax.fori_loop(0, 8, section, 0)
+    for cp in loads[2:]:
+        cp.start()
     mine = pltpu.make_async_copy(send.at[7, core], recv.at[me], own)
     mine.start()
 
@@ -264,7 +275,10 @@
     mid = jnp.zeros((16, LOCAL), F32)
     for q in range(4):
         hi, lo = split(lb[:, q * 256 : (q + 1) * 256])
-        mid = mid + mm(hi, dt[q, 0], NT) + mm(lo, dt[q, 0], NT) + mm(hi, dt[q, 1], NT)
+        at = OFFS[q] if q < 3 else OFFS[CH]
+        d_hi = dt[:, at : at + 256]
+        d_lo = dt[:, at + WIDTHS[q if q < 3 else CH] - 256 : at + WIDTHS[q if q < 3 else CH]]
+        mid = mid + mm(hi, d_hi, NT) + mm(lo, d_hi, NT) + mm(hi, d_lo, NT)
     mid_cross = mid[0:1] * mid[1:2] + mid[2:3] * mid[3:4]
     lb[...] = jnp.zeros_like(lb)
     for q in range(4):
@@ -283,7 +297,17 @@
             return total + tiles[q * 16 + t] * up
 
         total = lax.fori_loop(0, 16, put_mid, total)
-    qb[pl.ds(16, 8)] = jnp.broadcast_to(jnp.sum(total, axis=1, keepdims=True), (8, 128))
+    ms[...] = jnp.broadcast_to(jnp.sum(total, axis=1, keepdims=True), (8, 128))
+
+    def m_copy(k):
+        return pltpu.make_async_remote_copy(
+            src_ref=ms, dst_ref=mrecv.at[me], send_sem=mss.at[k], recv_sem=mrs.at[me],
+            device_id={"row": lax.rem(me + k, ROWS)}, device_id_type=MESH,
+        )
+
+    for k in range(1, ROWS):
+        m_copy(k).start()
+    mrecv[me] = ms[...]
 
     sign = jnp.where(lax.broadcasted_iota(jnp.int32, (16, 128), 1) < 64, 1.0, -1.0).astype(F32)
     mine.wait()
@@ -292,12 +316,15 @@
         for k in range(1, ROWS):
             arrival(c, lax.rem(me + k, ROWS)).wait_recv()
 
+        n = SIZES[c]
+
         def rows16(i, _):
-            at = pl.ds(pl.multiple_of(i * 16, 16), 16)
-            jat = pl.ds(pl.multiple_of(CR + i * 16, 16), 16)
-            coef = tw[pl.ds(pl.multiple_of(c * CR + i * 16, 16), 16)]
+            ats = [pl.ds(pl.multiple_of(2 * n * p + i * 16, 16), 16) for p in range(2 if n == 128 else 4)]
+            jats = [pl.ds(pl.multiple_of(2 * n * p + n + i * 16, 16), 16) for p in range(2 if n == 128 else 4)]
+            coef = tw[pl.ds(pl.multiple_of(STARTS[c] + i * 16, 16), 16)]
             for zu in range(2):
-                v = [recv[d, c, pl.ds(pl.multiple_of(zu * CR + i * 16, 16), 16)] for d in range(ROWS)]
+                at = pl.ds(pl.multiple_of(2 * STARTS[c] + zu * n + i * 16, 16), 16)
+                v = [recv[d, at] for d in range(ROWS)]
                 inner = [four(v[d0], v[d0 + 4], v[d0 + 8], v[d0 + 12], sign) for d0 in range(4)]
                 for f0 in range(4):
                     outs = four(*[turn(inner[d0][f0], d0 * f0, sign) for d0 in range(4)], sign)
@@ -310,15 +337,19 @@
                             ss = jnp.broadcast_to(coef[:, 2 * f + 1 : 2 * f + 2], (16, 128))
                             val, jval = val * cc + jval * ss, jval * cc - val * ss
                         cols = pl.ds(f * 256 + zu * 128, 128)
-                        yh[at, cols], yl[at, cols] = split(val)
-                        yh[jat, cols], yl[jat, cols] = split(jval)
+                        for p, (part, jpart) in enumerate(zip(split(val), split(jval))):
+                            for copy in range(p, len(ats), 2):
+                                yy[ats[copy], cols] = part
+                                yy[jats[copy], cols] = jpart
             return 0
 
-        lax.fori_loop(0, CR // 16, rows16, 0)
+        lax.fori_loop(0, n // 16, rows16, 0)
 
     def product(c, cols):
-        a, b = yh[:, cols], yl[:, cols]
-        return mm(dt[c, 0], a) + mm(dt[c, 0], b) + mm(dt[c, 1], a)
+        at, n = OFFS[c], SIZES[c]
+        if n == 128:
+            return mm(dt[:, at : at + 512], yy[pl.ds(0, 512), cols]) + mm(dt[:, at + 512 : at + 768], yy[pl.ds(0, 256), cols])
+        return mm(dt[:, at : at + 8 * n], yy[pl.ds(0, 8 * n), cols])
 
     for c in range(CH - 1):
         turned(c)
@@ -330,6 +361,13 @@
             return 0
 
         lax.fori_loop(0, 8, add, 0)
+    for k in range(1, ROWS):
+        d = lax.rem(me + k, ROWS)
+        pltpu.make_async_remote_copy(
+            src_ref=ms, dst_ref=mrecv.at[d], send_sem=mss.at[0], recv_sem=mrs.at[d],
+            device_id={"row": d}, device_id_type=MESH,
+        ).wait_recv()
+    middle = functools.reduce(lambda a, d: a + mrecv[d], range(1, ROWS), mrecv[0])
 
     turned(CH - 1)
 
@@ -356,7 +394,10 @@
         b = mm(weights, hi)
         return q + b[:16] + b[16:] + mm(weights[:16], lo)
 
-    qb[pl.ds(0, 16)] = lax.fori_loop(0, 16, contract, jnp.zeros((16, 128), F32))
+    q = lax.fori_loop(0, 16, contract, jnp.zeros((16, 128), F32), unroll=4)
+    q = q + pltpu.roll(q, 64, axis=1)
+    q = jnp.where(lane < 64, q[:8], q[8:])
+    qb[...] = jnp.where(jnp.logical_and(me == 0, lane == 64), middle, q) * SCALE
     mir[...] = exact(tiles[...].reshape(512, 128), flip).reshape(64, 8, 128)
 
     def join(t, _):
@@ -364,8 +405,7 @@
         pex[t] = (pex[t] + back) * SCALE
         return 0
 
-    lax.fori_loop(0, 64, join, 0)
-    qb[...] = qb[...] * SCALE
+    lax.fori_loop(0, 64, join, 0, unroll=8)
 
     def grp_copies(k):
         to = lax.rem(g + k, GRPS)
@@ -440,17 +480,13 @@
             cp.wait_recv()
     tile = functools.reduce(lambda a, d: a + r2[d], range(1, ROWS), r2[0])
     row_ref[...] = jnp.where(core == 0, tile, pltpu.roll(tile, 64, axis=1))[:, :64]
-    low = lax.broadcasted_iota(jnp.int32, (16, 128), 1) < 64
-    middle = functools.reduce(lambda a, d: a + q2[d, pl.ds(16, 8)], range(1, ROWS), q2[0, pl.ds(16, 8)])
     for m in range(8):
-        a, b = q2[2 * m, pl.ds(0, 16)], q2[2 * m + 1, pl.ds(0, 16)]
-        ab = jnp.where(low, a + pltpu.roll(a, 64, axis=1), b + pltpu.roll(b, 64, axis=1))
-        col_ref[:, pl.ds(m * 128, 128)] = ab[:8]
-        tiles[m] = ab[8:]
+        a, b = q2[2 * m], q2[2 * m + 1]
+        col_ref[:, pl.ds(m * 128, 128)] = jnp.where(lane < 64, a, pltpu.roll(b, 64, axis=1))
+        tiles[m] = jnp.where(lane < 64, pltpu.roll(a, 64, axis=1), b)
     mir[pl.ds(0, 8)] = exact(tiles[pl.ds(0, 8)].reshape(64, 128), flip).reshape(8, 8, 128)
     for t in range(8, 16):
-        first = middle if t == 8 else mir[16 - t]
-        col_ref[:, pl.ds(t * 128, 128)] = jnp.where(lane == 0, first, mir[15 - t])
+        col_ref[:, pl.ds(t * 128, 128)] = jnp.where(lane == 0, mir[(16 - t) % 8], mir[15 - t])
 
     for c in range(CH):
 
@@ -469,6 +505,7 @@
         lax.fori_loop(0, 8, drain, 0)
     for k in range(1, ROWS):
         b_copy(k).wait_send()
+        m_copy(k).wait_send()
         for cp in row_copies(k):
             cp.wait_send()
     for k in range(1, GRPS):
@@ -481,15 +518,15 @@
     dma = pltpu.SemaphoreType.DMA
     vm = pltpu.VMEM
     scratch = [
-        vm((2, LOCAL, L2), BF16), vm((2, 2, L2, 256), BF16), vm((CH, 2, LOCAL, 2 * CR), BF16),
+        vm((2, LOCAL, L2), BF16), vm((2, 2, L2, 256), BF16), vm((LOCAL, sum(WIDTHS)), BF16),
         vm((LOCAL, 128), F32), vm((64, 128), F32), vm((8, L1), F32), vm((8, L2), F32),
-        vm((8, 2, CH, 2 * CR, 128), F32), vm((ROWS, CH, 2 * CR, 128), F32),
-        vm((LOCAL, 4096), F32), vm((2 * CR, 4096), BF16), vm((2 * CR, 4096), BF16), vm((L1, 128), F32),
-        vm((8, 128), F32), vm((ROWS, 8, 128), F32), vm((16, 1024), F32), vm((8, 2048), F32),
-        vm((32, L1), BF16), vm((64, 8, 128), F32), vm((64, 8, 128), F32), vm((64, 8, 128), F32), vm((24, 128), F32),
-        vm((GRPS, 8, 8, 128), F32), vm((GRPS, 24, 128), F32), vm((8, 8, 128), F32), vm((ROWS, 8, 128), F32),
-        vm((24, 128), F32), vm((ROWS, 24, 128), F32),
-        dma((7,)), dma((2,)), dma((CH, ROWS)), dma((CH, ROWS)), dma, dma((ROWS,)), dma((ROWS,)),
+        vm((8, 2, 2 * LOCAL, 128), F32), vm((ROWS, 2 * LOCAL, 128), F32),
+        vm((LOCAL, 4096), F32), vm((512, 4096), BF16), vm((L1, 128), F32),
+        vm((8, 128), F32), vm((ROWS, 8, 128), F32), vm((8, 128), F32), vm((ROWS, 8, 128), F32), vm((16, 1024), F32), vm((8, 2048), F32),
+        vm((32, L1), BF16), vm((64, 8, 128), F32), vm((64, 8, 128), F32), vm((64, 8, 128), F32), vm((8, 128), F32),
+        vm((GRPS, 8, 8, 128), F32), vm((GRPS, 8, 128), F32), vm((8, 8, 128), F32), vm((ROWS, 8, 128), F32),
+        vm((8, 128), F32), vm((ROWS, 8, 128), F32),
+        dma((7,)), dma((2,)), dma((CH, ROWS)), dma((CH, ROWS)), dma, dma((ROWS,)), dma((ROWS,)), dma((ROWS,)), dma((ROWS,)),
         dma((GRPS,)), dma((GRPS,)), dma((GRPS,)), dma((GRPS,)),
         dma((ROWS,)), dma((ROWS,)), dma((ROWS,)), dma((ROWS,)),
     ]

time: 144 us -> 135 us (0.938)
  Pallas kernels: 140 us -> 132 us
    pallas_call x1, Pallas kernels: 140 us -> 132 us  [local(): pl.pallas_call(kernel, out_shape=(jax.ShapeDtypeStruct((HYPER, 64), F32),...]
where the time goes in v1:
time: 135 us
  Pallas kernels  132 us (98%)
  local copies, waits for them, and re-layouts  2.74 us (2%)
    pallas_call x1, Pallas kernels, local(): pl.pallas_call(kernel, out_shape=(jax.ShapeDtypeStruct((HYPER, 64), F32),...  132 us
    unnamed x2, local copies, waits for them, and re-layouts  2.74 us

profile of v1, /device:TPU:1, one launch (start us, length us, event | category | flops | bytes accessed | tf_op | source)
XLA Modules:
  0.0 135.0 jit_solution(13714421698364175474)
XLA Ops:
  0.6 131.6 %trace_terms.1 = (f32[8,64]{1,0:T(8,128)}, f32[8,2048]{1,0:T(8,128)}) custom-call(bf16[1,512,2048]{2,1,0:T(8,128)(2,1)} %z_hbm.1, bf16[1,512,2048]{2,1,0:T(8,128)(2,1)} %u_hbm.1, f32[8,8192]{1,0:T(8,128)} %rs_hbm.1, f32[8,2048]{1,0:T(8,128)} %cs_hbm.1, bf16[8,2,2048,256]{3,2,1,0:T(8,128)(2,1)} %constant.8.clone.w_hbm, ...), custom_call_target="tpu_custom_call" | custom-call | tf_op jit(solution)/shard_map/trace_terms/pallas_call | solution.py:534
  132.3 1.3 copy.12
  133.5 1.5 %copy.13 = f32[8,2048]{1,0:T(8,128)} copy(f32[8,2048]{1,0:T(8,128)} %get-tuple-element.5) | data formatting | bytes 131072

commit v2 on v1

--- a/solution.py
+++ b/solution.py
@@ -105,7 +105,7 @@
     row_ref, col_ref,
     x, wbuf, dt, tw, tb, rs, cs, send, recv, acc, yy, cross,
     bs, brecv, ms, mrecv, lb, upm, r32, tiles, mir, pex, qb, r1, q1, r2s, r2, q2s, q2,
-    lsem, wsem, ssem, rsem, own, bss, brs, mss, mrs, e1s, e1r, f1s, f1r, e2s, e2r, f2s, f2r,
+    xsem, lsem, wsem, ssem, rsem, own, bss, brs, mss, mrs, e1s, e1r, f1s, f1r, e2s, e2r, f2s, f2r,
 ):
     me, g = lax.axis_index("row"), lax.axis_index("grp")
     xh, y, core = me // 8, (me // 2) % 4, me % 2
@@ -123,18 +123,25 @@
     def w_copy(s, slot):
         return pltpu.make_async_copy(w_hbm.at[pair_of(s)], wbuf.at[slot], wsem.at[slot])
 
+    fields = []
+    for c in range(CH):
+        for zu, field in enumerate((z_hbm, u_hbm)):
+            at = pl.ds(2 * STARTS[c] + zu * SIZES[c], SIZES[c])
+            fields.append(
+                pltpu.make_async_copy(field.at[0, pl.ds(STARTS[c], SIZES[c])], x.at[at], xsem.at[2 * c + zu])
+            )
     loads = [
-        pltpu.make_async_copy(z_hbm.at[0], x.at[0], lsem.at[0]),
-        pltpu.make_async_copy(u_hbm.at[0], x.at[1], lsem.at[1]),
-        pltpu.make_async_copy(d_hbm, dt, lsem.at[2]),
-        pltpu.make_async_copy(tw_hbm, tw, lsem.at[3]),
-        pltpu.make_async_copy(tb_hbm.at[me], tb, lsem.at[4]),
-        pltpu.make_async_copy(rs_hbm, rs, lsem.at[5]),
-        pltpu.make_async_copy(cs_hbm, cs, lsem.at[6]),
+        pltpu.make_async_copy(d_hbm, dt, lsem.at[0]),
+        pltpu.make_async_copy(tw_hbm, tw, lsem.at[1]),
+        pltpu.make_async_copy(tb_hbm.at[me], tb, lsem.at[2]),
+        pltpu.make_async_copy(rs_hbm, rs, lsem.at[3]),
+        pltpu.make_async_copy(cs_hbm, cs, lsem.at[4]),
     ]
-    loads[0].start()
+    for cp in fields[:4]:
+        cp.start()
     w_copy(0, 0).start()
-    loads[1].start()
+    for cp in fields[4:]:
+        cp.start()
 
     def span(c):
         return pl.ds(2 * STARTS[c], 2 * SIZES[c])
@@ -161,44 +168,9 @@
         def _():
             block(7, 1 - core, c).start()
 
-    loads[0].wait()
-    loads[1].wait()
-    pl.semaphore_wait(barrier, ROWS - 1 + GRPS - 1)
-
-    def section(s, _):
-        slot = lax.rem(s, 2)
-        w_copy(s, slot).wait()
-
-        @pl.when(s < 7)
-        def _():
-            w_copy(s + 1, 1 - slot).start()
-
-        for zu in range(2):
-            got = mm(x[zu], wbuf[slot, 0]) + mm(x[zu], wbuf[slot, 1])
-            for t in range(2):
-                for c in range(CH):
-                    first, n = STARTS[c], SIZES[c]
-                    send[s, t, pl.ds(2 * first + zu * n, n)] = got[first : first + n, t * 128 : (t + 1) * 128]
-        start_block(s, 0)
-        return 0
-
-    lax.fori_loop(0, 8, section, 0)
-    for cp in loads[2:]:
-        cp.start()
-    mine = pltpu.make_async_copy(send.at[7, core], recv.at[me], own)
-    mine.start()
-
     lane = lax.broadcasted_iota(jnp.int32, (8, 128), 1)
     sub = lax.broadcasted_iota(jnp.int32, (128, 128), 0)
     lan = lax.broadcasted_iota(jnp.int32, (128, 128), 1)
-    parity = lax.broadcasted_iota(jnp.int32, (L2, 128), 0) % 2
-    alt = (1 - 2 * parity).astype(F32).astype(BF16)
-    for zu in range(2):
-        summed = mm(x[zu], alt)
-        for q in range(4):
-            bs[pl.ds(zu * 4 + q, 1)] = jnp.sum(
-                jnp.where(sub == lan, summed[q * 128 : (q + 1) * 128], 0.0), axis=0, keepdims=True
-            )
 
     def b_copy(k):
         return pltpu.make_async_remote_copy(
@@ -206,21 +178,91 @@
             device_id={"row": lax.rem(me + k, ROWS)}, device_id_type=MESH,
         )
 
-    for k in range(1, ROWS):
-        b_copy(k).start()
-    for c in range(1, CH):
+    def middle_sums():
+        parity = lax.broadcasted_iota(jnp.int32, (L2, 128), 0) % 2
+        alt = (1 - 2 * parity).astype(F32).astype(BF16)
+        summed = mm(x[...], alt)
+        for zu in range(2):
+            for q in range(4):
+                total = jnp.zeros((1, 128), F32)
+                for first, n in zip(STARTS, SIZES):
+                    if first // 128 == q:
+                        here = summed[2 * first + zu * n : 2 * first + zu * n + n]
+                        total = total + jnp.sum(
+                            jnp.where(sub[:n] + first % 128 == lan[:n], here, 0.0), axis=0, keepdims=True
+                        )
+                bs[pl.ds(zu * 4 + q, 1)] = total
+        for k in range(1, ROWS):
+            b_copy(k).start()
+
+    def drain(c, s, _):
+        @pl.when(s < 7)
+        def _():
+            block(s, 0, c).wait_send()
+            block(s, 1, c).wait_send()
+
+        @pl.when(s == 7)
+        def _():
+            block(7, 1 - core, c).wait_send()
+
+        return 0
+
+    for cp in fields:
+        cp.wait()
+    pl.semaphore_wait(barrier, ROWS - 1 + GRPS - 1)
+
+    def part(s, slot, first):
+        rows = x[pl.ds(first, LOCAL)]
+        got = mm(rows, wbuf[slot, 0]) + mm(rows, wbuf[slot, 1])
+        for t in range(2):
+            send[s, t, pl.ds(first, LOCAL)] = got[:, t * 128 : (t + 1) * 128]
+
+    def section(s, _):
+        slot = lax.rem(s, 2)
+        w_copy(s, slot).wait()
+        w_copy(s + 1, 1 - slot).start()
+        part(s, slot, 0)
+        part(s, slot, LOCAL)
+        block(s, 0, 0).start()
+        block(s, 1, 0).start()
+        return 0
+
+    w_copy(0, 0).wait()
+    w_copy(1, 1).start()
+    part(0, 0, 0)
+    part(0, 0, LOCAL)
+    block(0, 0, 0).start()
+    block(0, 1, 0).start()
+    section(1, 0)
+    middle_sums()
+    lax.fori_loop(2, 7, section, 0)
+    w_copy(7, 1).wait()
+    part(7, 1, 0)
+    part(7, 1, LOCAL)
+    block(7, 1 - core, 0).start()
+    for c in range(1, 3):
         lax.fori_loop(0, 8, lambda s, _, c=c: (start_block(s, c), 0)[1], 0)
-
-    for cp in loads[2:]:
+    for cp in loads:
+        cp.start()
+    mine = pltpu.make_async_copy(send.at[7, core], recv.at[me], own)
+    mine.start()
+
+
+    for cp in loads:
         cp.wait()
-    flip = (lax.rem(sub + lan, 128) == 0).astype(F32)
+    flip = (lax.rem(sub + lan, 128) == 0).astype(F32).astype(BF16)
+
+    def flipped(v):
+        hi, lo = split(v)
+        return mm(hi, flip) + mm(lo, flip)
+
 
     def stack_r(t, _):
         tiles[t] = rs[:, pl.ds(pl.multiple_of(t * 128, 128), 128)]
         return 0
 
     lax.fori_loop(0, 64, stack_r, 0)
-    mir[...] = exact(tiles[...].reshape(512, 128), flip).reshape(64, 8, 128)
+    mir[...] = flipped(tiles[...].reshape(512, 128)).reshape(64, 8, 128)
 
     def put_r(t, _):
         back = jnp.where(lane == 0, mir[lax.rem(64 - t, 64)], mir[63 - t])
@@ -242,7 +284,7 @@
     c_here = cs[:, pl.ds(pl.multiple_of(at * 128, 128), 128)]
     c_a = cs[:, pl.ds(pl.multiple_of((15 - at) * 128, 128), 128)]
     c_b = cs[:, pl.ds(pl.multiple_of(lax.rem(16 - at, 16) * 128, 128), 128)]
-    c_back = jnp.where(lane == 0, exact(c_b, flip), exact(c_a, flip))
+    c_back = jnp.where(lane == 0, flipped(c_b), flipped(c_a))
     c_back = own_half(c_back)
     c_back = jnp.where(jnp.logical_and(me == 0, lax.rem(lane, 64) == 0), 0.0, c_back)
     c_hi, c_lo = split(jnp.concatenate([own_half(c_here), c_back], axis=0))
@@ -308,6 +350,8 @@
     for k in range(1, ROWS):
         m_copy(k).start()
     mrecv[me] = ms[...]
+    for c in range(3, CH):
+        lax.fori_loop(0, 8, lambda s, _, c=c: (start_block(s, c), 0)[1], 0)
 
     sign = jnp.where(lax.broadcasted_iota(jnp.int32, (16, 128), 1) < 64, 1.0, -1.0).astype(F32)
     mine.wait()
@@ -380,7 +424,7 @@
             )
         return 0
 
-    lax.fori_loop(0, 8, finish, 0)
+    lax.fori_loop(0, 8, finish, 0, unroll=4)
 
     def contract(n, q):
         at = pl.ds(pl.multiple_of(n * 512, 512), 512)
@@ -394,18 +438,18 @@
         b = mm(weights, hi)
         return q + b[:16] + b[16:] + mm(weights[:16], lo)
 
-    q = lax.fori_loop(0, 16, contract, jnp.zeros((16, 128), F32), unroll=4)
+    q = lax.fori_loop(0, 16, contract, jnp.zeros((16, 128), F32), unroll=8)
     q = q + pltpu.roll(q, 64, axis=1)
     q = jnp.where(lane < 64, q[:8], q[8:])
     qb[...] = jnp.where(jnp.logical_and(me == 0, lane == 64), middle, q) * SCALE
-    mir[...] = exact(tiles[...].reshape(512, 128), flip).reshape(64, 8, 128)
+    mir[...] = flipped(tiles[...].reshape(512, 128)).reshape(64, 8, 128)
 
     def join(t, _):
         back = jnp.where(lane == 0, mir[lax.rem(64 - t, 64)], mir[63 - t])
         pex[t] = (pex[t] + back) * SCALE
         return 0
 
-    lax.fori_loop(0, 64, join, 0, unroll=8)
+    lax.fori_loop(0, 64, join, 0, unroll=16)
 
     def grp_copies(k):
         to = lax.rem(g + k, GRPS)
@@ -436,6 +480,8 @@
     for k in range(1, GRPS):
         for cp in grp_copies(k):
             cp.start()
+    for c in range(CH):
+        lax.fori_loop(0, 8, functools.partial(drain, c), 0)
     r1[g] = pex[pl.ds(g * 8, 8)]
     q1[g] = qb[...]
     for k in range(1, GRPS):
@@ -473,6 +519,12 @@
     for k in range(1, ROWS):
         for cp in row_copies(k):
             cp.start()
+    for k in range(1, ROWS):
+        b_copy(k).wait_send()
+        m_copy(k).wait_send()
+    for k in range(1, GRPS):
+        for cp in grp_copies(k):
+            cp.wait_send()
     r2[me] = r2s[me // 2]
     q2[me] = q2s[...]
     for k in range(1, ROWS):
@@ -484,32 +536,12 @@
         a, b = q2[2 * m], q2[2 * m + 1]
         col_ref[:, pl.ds(m * 128, 128)] = jnp.where(lane < 64, a, pltpu.roll(b, 64, axis=1))
         tiles[m] = jnp.where(lane < 64, pltpu.roll(a, 64, axis=1), b)
-    mir[pl.ds(0, 8)] = exact(tiles[pl.ds(0, 8)].reshape(64, 128), flip).reshape(8, 8, 128)
+    mir[pl.ds(0, 8)] = flipped(tiles[pl.ds(0, 8)].reshape(64, 128)).reshape(8, 8, 128)
     for t in range(8, 16):
         col_ref[:, pl.ds(t * 128, 128)] = jnp.where(lane == 0, mir[(16 - t) % 8], mir[15 - t])
 
-    for c in range(CH):
-
-        def drain(s, _, c=c):
-            @pl.when(s < 7)
-            def _():
-                block(s, 0, c).wait_send()
-                block(s, 1, c).wait_send()
-
-            @pl.when(s == 7)
-            def _():
-                block(7, 1 - core, c).wait_send()
-
-            return 0
-
-        lax.fori_loop(0, 8, drain, 0)
-    for k in range(1, ROWS):
-        b_copy(k).wait_send()
-        m_copy(k).wait_send()
+    for k in range(1, ROWS):
         for cp in row_copies(k):
-            cp.wait_send()
-    for k in range(1, GRPS):
-        for cp in grp_copies(k):
             cp.wait_send()
 
 
@@ -518,7 +550,7 @@
     dma = pltpu.SemaphoreType.DMA
     vm = pltpu.VMEM
     scratch = [
-        vm((2, LOCAL, L2), BF16), vm((2, 2, L2, 256), BF16), vm((LOCAL, sum(WIDTHS)), BF16),
+        vm((2 * LOCAL, L2), BF16), vm((2, 2, L2, 256), BF16), vm((LOCAL, sum(WIDTHS)), BF16),
         vm((LOCAL, 128), F32), vm((64, 128), F32), vm((8, L1), F32), vm((8, L2), F32),
         vm((8, 2, 2 * LOCAL, 128), F32), vm((ROWS, 2 * LOCAL, 128), F32),
         vm((LOCAL, 4096), F32), vm((512, 4096), BF16), vm((L1, 128), F32),
@@ -526,7 +558,7 @@
         vm((32, L1), BF16), vm((64, 8, 128), F32), vm((64, 8, 128), F32), vm((64, 8, 128), F32), vm((8, 128), F32),
         vm((GRPS, 8, 8, 128), F32), vm((GRPS, 8, 128), F32), vm((8, 8, 128), F32), vm((ROWS, 8, 128), F32),
         vm((8, 128), F32), vm((ROWS, 8, 128), F32),
-        dma((7,)), dma((2,)), dma((CH, ROWS)), dma((CH, ROWS)), dma, dma((ROWS,)), dma((ROWS,)), dma((ROWS,)), dma((ROWS,)),
+        dma((2 * CH,)), dma((5,)), dma((2,)), dma((CH, ROWS)), dma((CH, ROWS)), dma, dma((ROWS,)), dma((ROWS,)), dma((ROWS,)), dma((ROWS,)),
         dma((GRPS,)), dma((GRPS,)), dma((GRPS,)), dma((GRPS,)),
         dma((ROWS,)), dma((ROWS,)), dma((ROWS,)), dma((ROWS,)),
     ]

time: 135 us -> 134 us (level)
  no operation moved by 1% of the time
where the time goes in v2:
time: 134 us
  Pallas kernels  131 us (98%)
  local copies, waits for them, and re-layouts  2.74 us (2%)
    pallas_call x1, Pallas kernels, local(): pl.pallas_call(kernel, out_shape=(jax.ShapeDtypeStruct((HYPER, 64), F32),...  131 us
    unnamed x2, local copies, waits for them, and re-layouts  2.74 us

profile of v2, /device:TPU:1, one launch (start us, length us, event | category | flops | bytes accessed | tf_op | source)
XLA Modules:
  0.0 134.1 jit_solution(3649898153860567942)
XLA Ops:
  0.6 130.7 %trace_terms.1 = (f32[8,64]{1,0:T(8,128)}, f32[8,2048]{1,0:T(8,128)}) custom-call(bf16[1,512,2048]{2,1,0:T(8,128)(2,1)} %z_hbm.1, bf16[1,512,2048]{2,1,0:T(8,128)(2,1)} %u_hbm.1, f32[8,8192]{1,0:T(8,128)} %rs_hbm.1, f32[8,2048]{1,0:T(8,128)} %cs_hbm.1, bf16[8,2,2048,256]{3,2,1,0:T(8,128)(2,1)} %constant.8.clone.w_hbm, ...), custom_call_target="tpu_custom_call" | custom-call | tf_op jit(solution)/shard_map/trace_terms/pallas_call | solution.py:566
  131.3 1.3 copy.12
  132.6 1.5 %copy.13 = f32[8,2048]{1,0:T(8,128)} copy(f32[8,2048]{1,0:T(8,128)} %get-tuple-element.5) | data formatting | bytes 131072
